TPU v7x, 32 devices: a whole 2x2x4 slice. The times are simulated.
32 devices in a mesh: dp: 8 (over z, x), fsdp: 4 (over y, core).
Axes of the slice: x: 2, y: 2, z: 4, core: 2. Of those that a mesh axis runs over, the one named last changes fastest.
Arguments:
- block_input: bfloat16 [18432, 768], P(('dp', 'fsdp')), may hold values from -6 to 6
- cotangent: bfloat16 [18432, 768], P(('dp', 'fsdp')), may hold values from -6 to 6
- time_embed: bfloat16 [32, 128], P(('dp', 'fsdp')), may hold values from -6 to 6
- ada_weight: bfloat16 [128, 4608], P('fsdp'), may hold values from -0.25 to 0.25
- ada_bias: bfloat16 [4608], P('fsdp'), may hold values from -2 to 2
- attn_gain: bfloat16 [768], P('fsdp'), may hold values from 0.5 to 1.5
- qkv_weight: bfloat16 [768, 2304], P('fsdp'), may hold values from -0.21875 to 0.21875
- out_weight: bfloat16 [768, 768], P('fsdp'), may hold values from -0.875 to 0.875
- mlp_gain: bfloat16 [768], P('fsdp'), may hold values from 0.5 to 1.5
- up_weight: bfloat16 [768, 3072], P('fsdp'), may hold values from -0.21875 to 0.21875
- up_bias: bfloat16 [3072], P('fsdp'), may hold values from -2 to 2
- down_weight: bfloat16 [3072, 768], P('fsdp'), may hold values from -0.109375 to 0.109375
- down_bias: bfloat16 [768], P('fsdp'), may hold values from -2 to 2
Outputs:
- block_output: bfloat16 [18432, 768], P(('dp', 'fsdp'))
- input_grad: float32 [18432, 768], P(('dp', 'fsdp'))
- time_grad: float32 [32, 128], P(('dp', 'fsdp'))
- ada_weight_grad: float32 [128, 4608], P('fsdp')
- ada_bias_grad: float32 [4608], P('fsdp')
- attn_gain_grad: float32 [768], P('fsdp')
- qkv_weight_grad: float32 [768, 2304], P('fsdp')
- out_weight_grad: float32 [768, 768], P('fsdp')
- mlp_gain_grad: float32 [768], P('fsdp')
- up_weight_grad: float32 [768, 3072], P('fsdp')
- up_bias_grad: float32 [3072], P('fsdp')
- down_weight_grad: float32 [3072, 768], P('fsdp')
- down_bias_grad: float32 [768], P('fsdp')
All inputs are finite; a program needn't handle non-finite values.
Results may differ from a plain program's by a relative error of at most 0.015.
The roundings to bfloat16 on the way count: a program that leaves them out, or rounds other values in their place, can miss the bound.
Values may be sent and summed in bfloat16 or wider, within the bound.
No kernel may reach another device: no remote copies, remote signals or barrier semaphores. Data moves between devices by JAX's collectives and lax.ppermute only.
A program may use at most 192 MiB of HBM per device.

v0:
```python
from functools import partial
import jax
import jax.numpy as jnp
from jax import lax
from jax.sharding import PartitionSpec as P

HEAD_DIM = 64


def norm_modulate(values, gain, shift, scale):
    centre = jnp.mean(values, axis=-1, keepdims=True)
    centred = values - centre
    spread = jnp.mean(centred * centred, axis=-1, keepdims=True)
    return centred * lax.rsqrt(spread + 1e-05) * gain * (1.0 + scale) + shift


def rotary_tables(length, head_dim):
    half_dim = head_dim // 2
    position = jnp.arange(length).astype(jnp.float32)[:, None]
    frequency = 10000.0 ** (-2.0 * jnp.arange(half_dim).astype(jnp.float32) / head_dim)
    angles = position * frequency[None, :]
    return (jnp.cos(angles), jnp.sin(angles))


def rotate(tensor, cosines, sines):
    half_dim = tensor.shape[-1] // 2
    first = tensor[..., :half_dim]
    second = tensor[..., half_dim:]
    cos_b = cosines[:, None, :]
    sin_b = sines[:, None, :]
    return jnp.concatenate(
        [first * cos_b - second * sin_b, second * cos_b + first * sin_b], axis=-1
    )


def unrotate(tensor, cosines, sines):
    half_dim = tensor.shape[-1] // 2
    first = tensor[..., :half_dim]
    second = tensor[..., half_dim:]
    cos_b = cosines[:, None, :]
    sin_b = sines[:, None, :]
    return jnp.concatenate(
        [first * cos_b + second * sin_b, second * cos_b - first * sin_b], axis=-1
    )


def head_scores(query_h, key_h):
    return jnp.dot(query_h, key_h.T, preferred_element_type=jnp.float32) * HEAD_DIM ** (-0.5)


def attend_head(triple):
    query_h, key_h, value_h = triple
    scores = head_scores(query_h, key_h)
    row_max = jnp.max(scores, axis=-1, keepdims=True)
    shifted = jnp.exp(scores - row_max)
    row_total = jnp.sum(shifted, axis=-1, keepdims=True)
    weights = (shifted / row_total).astype(jnp.bfloat16)
    return (
        jnp.dot(weights, value_h, preferred_element_type=jnp.float32),
        row_max[:, 0],
        row_total[:, 0],
    )


def head_grads(items):
    query_h, key_h, value_h, grad_h, row_max, row_total = items
    scores = head_scores(query_h, key_h)
    probs = jnp.exp(scores - row_max[:, None]) / row_total[:, None]
    probs_low = probs.astype(jnp.bfloat16)
    value_grad = jnp.dot(probs_low.T, grad_h, preferred_element_type=jnp.float32)
    prob_grad = jnp.dot(grad_h, value_h.T, preferred_element_type=jnp.float32)
    score_grad = (probs * (prob_grad - jnp.sum(probs * prob_grad, axis=-1, keepdims=True))).astype(
        jnp.bfloat16
    )
    query_grad = jnp.dot(score_grad, key_h, preferred_element_type=jnp.float32) * HEAD_DIM ** (-0.5)
    key_grad = jnp.dot(score_grad.T, query_h, preferred_element_type=jnp.float32) * HEAD_DIM ** (
        -0.5
    )
    return (query_grad, key_grad, value_grad)


def run_forward(block32, cond, attn_set, mlp_set, cosines, sines):
    ada_weight, ada_bias, attn_gain, qkv_weight, out_weight = attn_set
    mlp_gain, up_weight, up_bias, down_weight, down_bias = mlp_set
    length, width = block32.shape
    heads = width // HEAD_DIM
    modulation = jnp.dot(cond, ada_weight, preferred_element_type=jnp.float32) + ada_bias.astype(
        jnp.float32
    )
    pieces = [modulation[:, index * width : (index + 1) * width] for index in range(6)]
    attn_in = norm_modulate(block32, attn_gain.astype(jnp.float32), pieces[0], pieces[1]).astype(
        jnp.bfloat16
    )
    qkv_proj = jnp.dot(attn_in, qkv_weight, preferred_element_type=jnp.float32)
    queries = (
        rotate(qkv_proj[:, :width].reshape(length, heads, HEAD_DIM), cosines, sines)
        .astype(jnp.bfloat16)
        .transpose(1, 0, 2)
    )
    keys = (
        rotate(qkv_proj[:, width : 2 * width].reshape(length, heads, HEAD_DIM), cosines, sines)
        .astype(jnp.bfloat16)
        .transpose(1, 0, 2)
    )
    values = (
        qkv_proj[:, 2 * width :]
        .reshape(length, heads, HEAD_DIM)
        .astype(jnp.bfloat16)
        .transpose(1, 0, 2)
    )
    head_out, row_max, row_total = lax.map(attend_head, (queries, keys, values))
    attended = head_out.transpose(1, 0, 2).reshape(length, width).astype(jnp.bfloat16)
    attn_branch = jnp.dot(attended, out_weight, preferred_element_type=jnp.float32)
    middle = block32 + pieces[2] * attn_branch
    mlp_in = norm_modulate(middle, mlp_gain.astype(jnp.float32), pieces[3], pieces[4]).astype(
        jnp.bfloat16
    )
    pre_act = jnp.dot(mlp_in, up_weight, preferred_element_type=jnp.float32) + up_bias.astype(
        jnp.float32
    )
    activ = jax.nn.gelu(pre_act, approximate=True).astype(jnp.bfloat16)
    mlp_branch = jnp.dot(activ, down_weight, preferred_element_type=jnp.float32) + down_bias.astype(
        jnp.float32
    )
    output = (middle + pieces[5] * mlp_branch).astype(jnp.bfloat16)
    saved = (
        modulation,
        attn_in,
        queries,
        keys,
        values,
        row_max,
        row_total,
        attended,
        attn_branch,
        middle,
        mlp_in,
        pre_act,
        activ,
        mlp_branch,
    )
    return (output, saved)


def local(
    block_input,
    cotangent,
    time_embed,
    ada_weight,
    ada_bias,
    attn_gain,
    qkv_weight,
    out_weight,
    mlp_gain,
    up_weight,
    up_bias,
    down_weight,
    down_bias,
):
    length, width = block_input.shape
    heads = width // HEAD_DIM
    cosines, sines = rotary_tables(length, HEAD_DIM)
    block32 = block_input.astype(jnp.float32)

    def gather_attention():
        return (
            lax.all_gather(ada_weight, "fsdp", axis=0, tiled=True),
            lax.all_gather(ada_bias, "fsdp", axis=0, tiled=True),
            lax.all_gather(attn_gain, "fsdp", axis=0, tiled=True),
            lax.all_gather(qkv_weight, "fsdp", axis=0, tiled=True),
            lax.all_gather(out_weight, "fsdp", axis=0, tiled=True),
        )

    def gather_feed():
        return (
            lax.all_gather(mlp_gain, "fsdp", axis=0, tiled=True),
            lax.all_gather(up_weight, "fsdp", axis=0, tiled=True),
            lax.all_gather(up_bias, "fsdp", axis=0, tiled=True),
            lax.all_gather(down_weight, "fsdp", axis=0, tiled=True),
            lax.all_gather(down_bias, "fsdp", axis=0, tiled=True),
        )

    attn_full = gather_attention()
    mlp_full = gather_feed()
    block_output, saved = run_forward(block32, time_embed, attn_full, mlp_full, cosines, sines)
    attn_back = gather_attention()
    mlp_back = gather_feed()
    unused_output, saved_back = run_forward(
        block32, time_embed, attn_back, mlp_back, cosines, sines
    )
    (
        modulation,
        attn_in,
        queries,
        keys,
        values,
        row_max,
        row_total,
        attended,
        attn_branch,
        middle,
        mlp_in,
        pre_act,
        activ,
        mlp_branch,
    ) = saved_back
    ada_full, ada_bias_full, attn_gain_full, qkv_full, out_full = attn_back
    mlp_gain_full, up_full, up_bias_full, down_full, down_bias_full = mlp_back
    pieces = [modulation[:, index * width : (index + 1) * width] for index in range(6)]
    grad32 = cotangent.astype(jnp.float32)
    mlp_grad = (pieces[5] * grad32).astype(jnp.bfloat16)
    gate_m_grad = jnp.sum(grad32 * mlp_branch, axis=0, keepdims=True)
    down_weight_grad = jnp.dot(activ.T, mlp_grad, preferred_element_type=jnp.float32)
    down_bias_grad = jnp.sum(mlp_grad.astype(jnp.float32), axis=0)
    activ_grad = jnp.dot(mlp_grad, down_full.T, preferred_element_type=jnp.float32)
    unused_act, gelu_back = jax.vjp(partial(jax.nn.gelu, approximate=True), pre_act)
    pre_grad = gelu_back(activ_grad)[0].astype(jnp.bfloat16)
    up_weight_grad = jnp.dot(mlp_in.T, pre_grad, preferred_element_type=jnp.float32)
    up_bias_grad = jnp.sum(pre_grad.astype(jnp.float32), axis=0)
    mlp_in_grad = jnp.dot(pre_grad, up_full.T, preferred_element_type=jnp.float32)
    unused_norm, norm_back_m = jax.vjp(
        norm_modulate, middle, mlp_gain_full.astype(jnp.float32), pieces[3], pieces[4]
    )
    middle_part, mlp_gain_grad, shift_m_grad, scale_m_grad = norm_back_m(mlp_in_grad)
    middle_grad = grad32 + middle_part
    mlp_shares = (
        lax.psum_scatter(
            mlp_gain_grad.astype(jnp.bfloat16), "fsdp", scatter_dimension=0, tiled=True
        ).astype(jnp.float32),
        lax.psum_scatter(
            up_weight_grad.astype(jnp.bfloat16), "fsdp", scatter_dimension=0, tiled=True
        ).astype(jnp.float32),
        lax.psum_scatter(
            up_bias_grad.astype(jnp.bfloat16), "fsdp", scatter_dimension=0, tiled=True
        ).astype(jnp.float32),
        lax.psum_scatter(
            down_weight_grad.astype(jnp.bfloat16), "fsdp", scatter_dimension=0, tiled=True
        ).astype(jnp.float32),
        lax.psum_scatter(
            down_bias_grad.astype(jnp.bfloat16), "fsdp", scatter_dimension=0, tiled=True
        ).astype(jnp.float32),
    )
    attn_grad = (pieces[2] * middle_grad).astype(jnp.bfloat16)
    gate_a_grad = jnp.sum(middle_grad * attn_branch, axis=0, keepdims=True)
    out_weight_grad = jnp.dot(attended.T, attn_grad, preferred_element_type=jnp.float32)
    attended_grad = jnp.dot(attn_grad, out_full.T, preferred_element_type=jnp.float32).astype(
        jnp.bfloat16
    )
    grad_heads = attended_grad.reshape(length, heads, HEAD_DIM).transpose(1, 0, 2)
    query_grad, key_grad, value_grad = lax.map(
        head_grads, (queries, keys, values, grad_heads, row_max, row_total)
    )
    query_grad = unrotate(query_grad.transpose(1, 0, 2), cosines, sines).reshape(length, width)
    key_grad = unrotate(key_grad.transpose(1, 0, 2), cosines, sines).reshape(length, width)
    value_grad = value_grad.transpose(1, 0, 2).reshape(length, width)
    qkv_grad = jnp.concatenate([query_grad, key_grad, value_grad], axis=1).astype(jnp.bfloat16)
    qkv_weight_grad = jnp.dot(attn_in.T, qkv_grad, preferred_element_type=jnp.float32)
    attn_in_grad = jnp.dot(qkv_grad, qkv_full.T, preferred_element_type=jnp.float32)
    unused_first, norm_back_a = jax.vjp(
        norm_modulate, block32, attn_gain_full.astype(jnp.float32), pieces[0], pieces[1]
    )
    input_part, attn_gain_grad, shift_a_grad, scale_a_grad = norm_back_a(attn_in_grad)
    input_grad = middle_grad + input_part
    modulation_grad = jnp.concatenate(
        [shift_a_grad, scale_a_grad, gate_a_grad, shift_m_grad, scale_m_grad, gate_m_grad], axis=1
    ).astype(jnp.bfloat16)
    ada_weight_grad = jnp.dot(time_embed.T, modulation_grad, preferred_element_type=jnp.float32)
    ada_bias_grad = modulation_grad.astype(jnp.float32)[0]
    time_grad = jnp.dot(modulation_grad, ada_full.T, preferred_element_type=jnp.float32)
    attn_shares = (
        lax.psum_scatter(
            ada_weight_grad.astype(jnp.bfloat16), "fsdp", scatter_dimension=0, tiled=True
        ).astype(jnp.float32),
        lax.psum_scatter(
            ada_bias_grad.astype(jnp.bfloat16), "fsdp", scatter_dimension=0, tiled=True
        ).astype(jnp.float32),
        lax.psum_scatter(
            attn_gain_grad.astype(jnp.bfloat16), "fsdp", scatter_dimension=0, tiled=True
        ).astype(jnp.float32),
        lax.psum_scatter(
            qkv_weight_grad.astype(jnp.bfloat16), "fsdp", scatter_dimension=0, tiled=True
        ).astype(jnp.float32),
        lax.psum_scatter(
            out_weight_grad.astype(jnp.bfloat16), "fsdp", scatter_dimension=0, tiled=True
        ).astype(jnp.float32),
    )
    totals = lax.psum(
        (
            mlp_shares[0],
            mlp_shares[1],
            mlp_shares[2],
            mlp_shares[3],
            mlp_shares[4],
            attn_shares[0],
            attn_shares[1],
            attn_shares[2],
            attn_shares[3],
            attn_shares[4],
        ),
        "dp",
    )
    mlp_sums = totals[:5]
    attn_sums = totals[5:]
    return (
        block_output,
        input_grad,
        time_grad,
        attn_sums[0],
        attn_sums[1],
        attn_sums[2],
        attn_sums[3],
        attn_sums[4],
        mlp_sums[0],
        mlp_sums[1],
        mlp_sums[2],
        mlp_sums[3],
        mlp_sums[4],
    )


def solution(mesh):
    return jax.shard_map(
        local,
        mesh=mesh,
        in_specs=(
            P(("dp", "fsdp"), None),
            P(("dp", "fsdp"), None),
            P(("dp", "fsdp"), None),
            P("fsdp", None),
            P("fsdp"),
            P("fsdp"),
            P("fsdp", None),
            P("fsdp", None),
            P("fsdp"),
            P("fsdp", None),
            P("fsdp"),
            P("fsdp", None),
            P("fsdp"),
        ),
        out_specs=(
            P(("dp", "fsdp"), None),
            P(("dp", "fsdp"), None),
            P(("dp", "fsdp"), None),
            P("fsdp", None),
            P("fsdp"),
            P("fsdp"),
            P("fsdp", None),
            P("fsdp", None),
            P("fsdp"),
            P("fsdp", None),
            P("fsdp"),
            P("fsdp", None),
            P("fsdp"),
        ),
        check_vma=False,
    )
```

profile of v0, /device:TPU:0, one launch (start us, length us, event | category | flops | bytes accessed | tf_op | source)
XLA Modules:
  0.0 819.6 jit_solution(13222286501110139619)
XLA Ops:
  15.5 8.9 %all-reduce.10 = (bf16[768]{0:T(1024)(128)(2,1)S(1)}, bf16[768]{0:T(1024)(128)(2,1)S(1)}, bf16[768]{0:T(1024)(128)(2,1)S(1)}) all-reduce(bf16[768]{0:T(1024)(128)(2,1)S(1)} %dynamic-update-slice, bf16[768]{0:T(1024)(128)(2,1)S(1)} %dynamic-update-slice.2, bf16[768]{0:T(1024)(128)(2,1)S(1)} %dynamic-update-slice.1), channel_id=1, replica_groups=mesh['dp'=8,'fsdp'=4] {'fsdp'}, use_global_device_ids=true, to_apply=%add | all-reduce | flops 2304 | bytes 9216
  26.4 5.2 all-gather.1
  32.2 5.4 all-gather
  40.4 21.9 %all-gather.10.cloned.1.call-done = bf16[768,2304]{1,0:T(8,128)(2,1)} async-done(((bf16[192,2304]{1,0:T(8,128)(2,1)}), bf16[768,2304]{1,0:T(8,128)(2,1)}) %all-gather.10.cloned.1.call-update) | async-done | bytes 3538960 | tf_op jit(solution)/shard_map/all_gather | solution.py:170
  62.4 4.5 fusion.109
  67.0 2.0 fusion.117
  72.2 2.6 copy.57
  74.8 2.8 copy.52
  77.6 2.0 subtract_convert_fusion.2
  83.1 2.6 copy.56
  85.7 74.1 %while.42 = (s32[]{:T(128)}, bf16[12,576,64]{1,2,0:T(8,128)(2,1)}, f32[12,576]{1,0:T(8,128)}, f32[12,576]{1,0:T(8,128)}, bf16[12,576,64]{2,1,0:T(8,128)(2,1)S(1)...) while((s32[]{:T(128)}, bf16[12,576,64]{1,2,0:T(8,128)(2,1)}, ...), condition=%wide.region_11.12_spmd.clone, body=%wide.region_8.0_spmd.sunk.clone | while | flops 87255936 | bytes 4619613 | solution.py:111
  118.0 1.9 fusion.191
  130.4 2.0 fusion.191
  136.6 1.9 fusion.191
  155.1 2.0 fusion.191
  161.0 3.7 fusion.114
  165.7 7.6 fusion.112
  173.3 11.7 %fusion.121 = (bf16[3072]{0:T(1024)(128)(2,1)}, bf16[576,3072]{1,0:T(8,128)(2,1)S(1)}) fusion(f32[576,3072]{1,0:T(8,128)} %fusion.112, f32[3072]{0:T(1024)} %bitcast.202, bf16[3072,768]{1,0:T(8,128)(2,1)} %all-gather.16.cloned.1.call-done, bf16[576,768]{1,0:T(8,128)(2,1)S(1)} %copy-done.9, f32[768]{0:T(1024)} %get-tuple-element.214), kind=kOutput, calls=%fused_computation.198 | convolution fusion | flops 2758161408 | bytes 16241664 | tf_op jit(solution)/shard_map/dot_general | solution.py:215
  185.0 4.0 multiply_reduce_fusion.1
  191.2 2.3 convolution_convert_fusion.3
  193.4 3.7 convolution_convert_fusion.4
  197.1 2.3 copy.61
  199.4 113.5 %while.43 = (s32[]{:T(128)}, f32[12,576,64]{1,2,0:T(8,128)}, f32[12,576,64]{1,2,0:T(8,128)}, bf16[12,576,64]{1,2,0:T(8,128)(2,1)}, bf16[12,576,64]{2,1,0:T(8,128...) while((s32[]{:T(128)}, f32[12,576,64]{1,2,0:T(8,128)}, ...), condition=%wide.region_18.19_spmd.clone, body=%wide.region_16.18_spmd.sunk.clone | while | flops 215395776 | bytes 11369585 | solution.py:250
  205.0 1.9 fusion.202
  214.5 1.9 fusion.202
  223.9 1.9 fusion.202
  233.4 1.9 fusion.202
  242.9 1.9 fusion.202
  252.3 1.9 fusion.202
  261.8 1.9 fusion.202
  271.2 1.9 fusion.202
  280.7 1.9 fusion.202
  290.1 1.9 fusion.202
  299.6 1.9 fusion.202
  309.1 1.9 fusion.202
  313.0 2.8 add_convert_fusion.4
  317.4 2.8 fusion.78
  322.0 3.1 multiply_reduce_fusion.3
  329.3 9.4 %fusion.76 = bf16[768]{0:T(1024)(128)(2,1)} fusion(bf16[576,768]{1,0:T(8,128)(2,1)S(1)} %copy-done.9, bf16[3072,768]{1,0:T(8,128)(2,1)} %all-gather.16.cloned.1.call-done, f32[768]{0:T(1024)} %convert_element_type.257, f32[576,3072]{1,0:T(8,128)} %fusion.112, f32[3072]{0:T(1024)} %bitcast.203), kind=kOutput, calls=%fused_computation.110 | convolution fusion | flops 2737372416 | bytes 12698112 | tf_op jit(solution)/shard_map/dot_general | solution.py:122
  341.5 6.9 convolution_convert_fusion
  349.1 7.9 convolution_convert_fusion.2
  360.1 10.5 %convolution_convert_fusion.1 = bf16[3072,768]{1,0:T(8,128)(2,1)} fusion(bf16[576,768]{1,0:T(8,128)(2,1)S(1)} %copy-done.9, f32[768]{0:T(1024)S(1)} %copy-done.32, f32[576,3072]{1,0:T(8,128)} %fusion.112, f32[3072]{0:T(1024)S(1)} %bitcast.204), kind=kOutput, calls=%fused_computation.84 | convolution fusion | flops 2739290112 | bytes 12696576 | tf_op jit(solution)/shard_map/dot_general | solution.py:213
  371.8 35.5 %while.41 = (s32[]{:T(128)}, bf16[12,576,64]{1,2,0:T(8,128)(2,1)S(1)}, bf16[12,576,64]{2,1,0:T(8,128)(2,1)}, bf16[12,576,64]{2,1,0:T(8,128)(2,1)}, bf16[12,576,64]{2,1,0:T(8,128)(2,1)}) while((s32[]{:T(128)}, bf16[12,576,64]{1,2,0:T(8,128)(2,1)S(1)}, bf16[12,576,64]{2,1,0:T(8,128)(2,1)}, bf16[12,576,64]{2,1,0:T(8,128)(2,1)}, ...), condition=%wide.region_5.6_spmd.clone, body=%wide.region_2.5_spmd.sunk.clone | while | flops 87255936 | bytes 4752197 | solution.py:111
  409.9 11.0 %all-reduce.9 = (bf16[4608]{0:T(1024)(128)(2,1)S(1)}, bf16[768]{0:T(1024)(128)(2,1)S(1)}, bf16[768]{0:T(1024)(128)(2,1)S(1)}, bf16[3072]{0:T(1024)(128)(2,1)S(1)}, bf16[768]{0:T(1024)(128)(2,1)S(1)}) all-reduce(bf16[4608]{0:T(1024)(128)(2,1)S(1)} %dynamic-update-slice.8, ...), channel_id=3, replica_groups=mesh['dp'=8,'fsdp'=4] {'fsdp'}, use_global_device_ids=true, to_apply=%region_29.30.clone | all-reduce | flops 9984 | bytes 39936
  422.3 12.3 %add_convert_fusion.1 = bf16[576,768]{1,0:T(8,128)(2,1)} fusion(f32[576,768]{1,0:T(8,128)} %copy-done.10, bf16[3072,768]{1,0:T(8,128)(2,1)} %all-gather.16.cloned.1.call-done, bf16[768,3072]{1,0:T(8,128)(2,1)} %all-gather.14.cloned.1.call-done, f32[3072]{0:T(1024)S(1)} %bitcast.205, f32[768]{0:T(1024)S(1)} %copy-done.46, f32[768]{0:T(1024)S(1)} %copy-done.48, ...), kind=kOutput, calls=%fused_computation.122 | convolution fusion | flops 5457936384 | bytes 12123648 | tf_op jit(solution)/shard_map/dot_general | solution.py:122
  434.6 26.3 %reduce-scatter.12.cloned.1.call-done = bf16[192,3072]{1,0:T(8,128)(2,1)} async-done(((bf16[768,3072]{1,0:T(8,128)(2,1)}), bf16[192,3072]{1,0:T(8,128)(2,1)}) %reduce-scatter.12.cloned.1.call-update) | async-done | bytes 1179664 | tf_op jit(solution)/shard_map/reduce_scatter | solution.py:230
  460.9 50.4 %reduce-scatter.14.cloned.1.call-done = bf16[768,768]{1,0:T(8,128)(2,1)} async-done(((bf16[3072,768]{1,0:T(8,128)(2,1)}), bf16[768,768]{1,0:T(8,128)(2,1)}) %reduce-scatter.14.cloned.1.call-update) | async-done | bytes 1179664 | tf_op jit(solution)/shard_map/reduce_scatter | solution.py:236
  511.3 301.2 %all-reduce.12 = (f32[32,4608]{1,0:T(8,128)}, f32[1152]{0:T(1024)}, f32[192]{0:T(256)}, f32[192,2304]{1,0:T(8,128)}, f32[192,768]{1,0:T(8,128)}, /*index=5*/f32[...) all-reduce(bf16[32,4608]{1,0:T(8,128)(2,1)} %reduce-scatter.6.clone, ...), channel_id=1, replica_groups=mesh['dp'=8,'fsdp'=4] {'dp'}, use_global_device_ids=true, to_apply=%region_28.29 | all-reduce | flops 1919424 | bytes 11521536 | tf_op jit(solution)/shard_map/psum | solution.py:287
  (406 shorter events, 232.1 us)
Async XLA Ops:
  7.2 30.9 %all-gather.8.cloned.1.call-start = ((), (), s32[]{:S(2)}) async-start(), calls=%async_computation.5 | async-start | bytes 1474560 | tf_op jit(solution)/shard_map/all_gather | solution.py:167
  7.9 54.4 %all-gather.10.cloned.1.call-start = ((), (), s32[]{:S(2)}) async-start(), calls=%async_computation.6 | async-start | bytes 4423680 | tf_op jit(solution)/shard_map/all_gather | solution.py:170
  8.7 151.1 %all-gather.12.cloned.1.call-start = ((), (), s32[]{:S(2)}) async-start(), calls=%async_computation.7 | async-start | bytes 1474560 | tf_op jit(solution)/shard_map/all_gather | solution.py:171
  9.4 156.2 %all-gather.14.cloned.1.call-start = ((), (), s32[]{:S(2)}) async-start(), calls=%async_computation.8 | async-start | bytes 5898240 | tf_op jit(solution)/shard_map/all_gather | solution.py:177
  10.0 163.3 %all-gather.16.cloned.1.call-start = ((), (), s32[]{:S(2)}) async-start(), calls=%async_computation.9 | async-start | bytes 5898240 | tf_op jit(solution)/shard_map/all_gather | solution.py:179
  10.6 424.1 %reduce-scatter.10.cloned.1.call-start = ((), (), s32[]{:S(2)}) async-start(), calls=%async_computation.12 | async-start | bytes 1474560 | tf_op jit(solution)/shard_map/reduce_scatter | solution.py:283
  10.8 2.8 copy-start.50
  10.8 4.0 copy-start.56
  10.8 4.3 copy-start.57
  10.8 4.5 copy-start.58
  10.8 13.6 %copy-start.51 = (bf16[768]{0:T(1024)(128)(2,1)S(1)}, bf16[768]{0:T(1024)(128)(2,1)}, u32[]{:S(2)}) copy-start(bf16[768]{0:T(1024)(128)(2,1)} %param.29) | copy-start | bytes 4612
  10.9 14.9 %copy-start = (bf16[576,768]{1,0:T(8,128)(2,1)S(1)}, bf16[576,768]{1,0:T(8,128)(2,1)}, u32[]{:S(2)}) copy-start(bf16[576,768]{1,0:T(8,128)(2,1)} %param.19) | copy-start | bytes 2654212
  12.0 14.3 %copy-start.47 = (bf16[1152]{0:T(1024)(128)(2,1)S(1)}, bf16[1152]{0:T(1024)(128)(2,1)}, u32[]{:S(2)}) copy-start(bf16[1152]{0:T(1024)(128)(2,1)} %param.23) | copy-start | bytes 6916
  24.5 42.3 %copy-start.17 = (f32[768]{0:T(1024)}, f32[768]{0:T(1024)S(1)}, u32[]{:S(2)}) copy-start(f32[768]{0:T(1024)S(1)} %convert_element_type.245) | copy-start | bytes 9220
  26.3 40.5 %copy-start.23 = (f32[576]{0:T(1024)}, f32[576]{0:T(1024)S(1)}, u32[]{:S(2)}) copy-start(f32[576]{0:T(1024)S(1)} %fusion.77) | copy-start | bytes 6916
  26.4 40.5 %copy-start.19 = (f32[576]{0:T(1024)}, f32[576]{0:T(1024)S(1)}, u32[]{:S(2)}) copy-start(f32[576]{0:T(1024)S(1)} %fusion.97) | copy-start | bytes 6916
  38.0 39.6 %copy-start.15 = (f32[576,32]{0,1:T(8,128)}, f32[576,32]{0,1:T(8,128)S(1)}, u32[]{:S(2)}) copy-start(f32[576,32]{0,1:T(8,128)S(1)} %get-tuple-element.313) | copy-start | bytes 221188
  38.0 39.6 %copy-start.16 = (f32[576,32]{0,1:T(8,128)}, f32[576,32]{0,1:T(8,128)S(1)}, u32[]{:S(2)}) copy-start(f32[576,32]{0,1:T(8,128)S(1)} %get-tuple-element.314) | copy-start | bytes 221188
  40.4 26.4 %copy-start.21 = (f32[768]{0:T(1024)}, f32[768]{0:T(1024)S(1)}, u32[]{:S(2)}) copy-start(f32[768]{0:T(1024)S(1)} %get-tuple-element.218) | copy-start | bytes 9220
  40.4 26.4 %copy-start.49 = (f32[768]{0:T(1024)}, f32[768]{0:T(1024)S(1)}, u32[]{:S(2)}) copy-start(f32[768]{0:T(1024)S(1)} %get-tuple-element.217) | copy-start | bytes 9220
  40.4 120.5 %copy-start.33 = (f32[768]{0:T(1024)}, f32[768]{0:T(1024)S(1)}, u32[]{:S(2)}) copy-start(f32[768]{0:T(1024)S(1)} %get-tuple-element.219) | copy-start | bytes 9220
  165.6 7.6 copy-start.9
  173.3 11.7 %copy-start.28 = (f32[576]{0:T(1024)S(1)}, f32[576]{0:T(1024)}, u32[]{:S(2)}) copy-start(f32[576]{0:T(1024)} %copy-done.27) | copy-start | bytes 6916
  173.3 11.7 %copy-start.36 = (f32[768]{0:T(1024)S(1)}, f32[768]{0:T(1024)}, u32[]{:S(2)}) copy-start(f32[768]{0:T(1024)} %convert_element_type.253) | copy-start | bytes 9220
  173.3 11.7 %copy-start.38 = (f32[576]{0:T(1024)S(1)}, f32[576]{0:T(1024)}, u32[]{:S(2)}) copy-start(f32[576]{0:T(1024)} %fusion.98) | copy-start | bytes 6916
  173.3 11.7 %copy-start.39 = (f32[768]{0:T(1024)S(1)}, f32[768]{0:T(1024)}, u32[]{:S(2)}) copy-start(f32[768]{0:T(1024)} %get-tuple-element.216) | copy-start | bytes 9220
  173.3 11.7 %copy-start.54 = (bf16[768,3072]{1,0:T(8,128)(2,1)S(1)}, bf16[768,3072]{1,0:T(8,128)(2,1)}, u32[]{:S(2)}) copy-start(bf16[768,3072]{1,0:T(8,128)(2,1)} %all-gather.14.cloned.1.call-done) | copy-start | bytes 14155780
  185.0 4.1 copy-start.59
  185.0 4.1 copy-start.26
  312.9 121.7 %reduce-scatter.6.cloned.1.call-start = ((), (), s32[]{:S(2)}) async-start(), calls=%async_computation.10 | async-start | bytes 1474560 | tf_op jit(solution)/shard_map/reduce_scatter | solution.py:271
  312.9 3.2 copy-start.55
  316.0 4.2 copy-start.13
  316.1 4.1 copy-start.14
  317.4 2.8 copy-start.24
  317.4 2.9 copy-start.20
  317.4 4.6 copy-start.6
  341.5 93.2 %reduce-scatter.8.cloned.1.call-start = ((), (), s32[]{:S(2)}) async-start(), calls=%async_computation.11 | async-start | bytes 4423680 | tf_op jit(solution)/shard_map/reduce_scatter | solution.py:280
  348.5 112.4 %reduce-scatter.12.cloned.1.call-start = ((), (), s32[]{:S(2)}) async-start(), calls=%async_computation.13 | async-start | bytes 5898240 | tf_op jit(solution)/shard_map/reduce_scatter | solution.py:230
  357.0 3.0 copy-start.41
  357.1 154.2 %reduce-scatter.14.cloned.1.call-start = ((), (), s32[]{:S(2)}) async-start(), calls=%async_computation.14 | async-start | bytes 5898240 | tf_op jit(solution)/shard_map/reduce_scatter | solution.py:236
  371.8 35.5 %copy-start.11 = (bf16[768,768]{1,0:T(8,128)(2,1)S(1)}, bf16[768,768]{1,0:T(8,128)(2,1)}, u32[]{:S(2)}) copy-start(bf16[768,768]{1,0:T(8,128)(2,1)} %all-gather.12.cloned.1.call-done) | copy-start | bytes 3538948
  371.8 35.5 %copy-start.35 = (f32[768]{0:T(1024)S(1)}, f32[768]{0:T(1024)}, u32[]{:S(2)}) copy-start(f32[768]{0:T(1024)} %copy-done.33) | copy-start | bytes 9220
  408.4 13.0 %copy-start.7 = (bf16[128,4608]{1,0:T(8,128)(2,1)S(1)}, bf16[128,4608]{1,0:T(8,128)(2,1)}, u32[]{:S(2)}) copy-start(bf16[128,4608]{1,0:T(8,128)(2,1)} %all-gather.8.cloned.1.call-done) | copy-start | bytes 3538948
  408.4 13.9 %copy-start.37 = (f32[768]{0:T(1024)S(1)}, f32[768]{0:T(1024)}, u32[]{:S(2)}) copy-start(f32[768]{0:T(1024)} %convert_element_type.253) | copy-start | bytes 9220
  408.4 13.9 %copy-start.40 = (f32[768]{0:T(1024)S(1)}, f32[768]{0:T(1024)}, u32[]{:S(2)}) copy-start(f32[768]{0:T(1024)} %get-tuple-element.216) | copy-start | bytes 9220
  408.4 13.9 %copy-start.42 = (f32[4,1,768]{2,1,0:T(1,128)S(1)}, f32[4,1,768]{2,1,0:T(1,128)}, u32[]{:S(2)}) copy-start(f32[4,1,768]{2,1,0:T(1,128)} %convert_element_type.288) | copy-start | bytes 36868
  408.4 13.9 %copy-start.46 = (f32[768]{0:T(1024)S(1)}, f32[768]{0:T(1024)}, u32[]{:S(2)}) copy-start(f32[768]{0:T(1024)} %convert_element_type.257) | copy-start | bytes 9220
  408.4 13.9 %copy-start.48 = (f32[768]{0:T(1024)S(1)}, f32[768]{0:T(1024)}, u32[]{:S(2)}) copy-start(f32[768]{0:T(1024)} %get-tuple-element.215) | copy-start | bytes 9220
  (22 other events, 32.9 us)
Sparse Core Ops, SparseCore 0:
  9.5 20.2 all-gather.7
  31.4 30.9 all-gather.9
  63.9 17.3 all-gather.11
  82.8 37.4 all-gather.13
  121.6 37.4 all-gather.15
  313.0 25.5 reduce-scatter.9
  341.8 25.6 reduce-scatter.5
  370.0 40.3 reduce-scatter.7
  412.9 47.9 reduce-scatter.11
  463.3 47.9 reduce-scatter.13
where the time goes:
time: 827 us; the launch traced here: 820 us
  blocking collectives  332 us (40%)
  matrix products  264 us (32%)
  waiting for transfers between devices  102 us (12%)
  local copies, waits for them, and re-layouts  74.4 us (9%)
  other arithmetic  28.6 us (3%)
  between operations  17.8 us (2%)
    psum x1, blocking collectives, local(): lax.psum((mlp_shares[0], mlp_shares[1], mlp_shares[2], mlp_shares[3], mlp...  301 us
    reduce_scatter x1, waiting for transfers between devices, local(): lax.psum_scatter(down_weight_grad.astype(jnp.bfloat16), 'fsdp', scatter_d...  50.4 us
    dot_general x36, matrix products, head_scores(): jnp.dot(query_h, key_h.T, preferred_element_type=jnp.float32)  50.3 us
    dot_general x24, matrix products, attend_head(): jnp.dot(weights, value_h, preferred_element_type=jnp.float32)  38.9 us
    dynamic_update_slice x24, local copies, waits for them, and re-layouts, run_forward(): head_out, row_max, row_total = lax.map(attend_head, (queries, keys, values))  32.2 us
    reduce_scatter x1, waiting for transfers between devices, local(): lax.psum_scatter(up_weight_grad.astype(jnp.bfloat16), 'fsdp', scatter_dim...  26.3 us
    dot_general x12, matrix products, head_grads(): jnp.dot(score_grad.T, query_h, preferred_element_type=jnp.float32)  23.3 us
    dot_general x12, matrix products, head_grads(): jnp.dot(probs_low.T, grad_h, preferred_element_type=jnp.float32)  22.6 us
  transfers between devices with their start and end apart: 10, of which 3 were waited for; matrix products, arithmetic and copies ran while one was open for 27% of the time, Pallas kernels for 0%

commit v1 on v0

--- a/solution.py
+++ b/solution.py
@@ -5,6 +5,28 @@
 from jax.sharding import PartitionSpec as P
 
 HEAD_DIM = 64
+
+
+def joined_along(blocks, dim):
+    lengths = list(blocks.shape[1:])
+    lengths[dim] *= blocks.shape[0]
+    return jnp.moveaxis(blocks, 0, dim).reshape(lengths)
+
+
+def collect(shard, axis, dim):
+    length = lax.axis_size(axis)
+    pairs = [(i, (i + 1) % length) for i in range(length)]
+    back = [(b, a) for a, b in pairs]
+    lower, upper = ([], [])
+    for lap in range(length - 1):
+        if lap % 2 == 0:
+            lower.append(lax.ppermute(lower[-1] if lower else shard, axis, pairs))
+        else:
+            upper.append(lax.ppermute(upper[-1] if upper else shard, axis, back))
+    tiles = jnp.stack([*lower[::-1], shard, *upper])
+    shift = lax.axis_index(axis) - len(lower)
+    tiles = tiles[(jnp.arange(length) - shift) % length]
+    return joined_along(tiles, dim)
 
 
 def norm_modulate(values, gain, shift, scale):
@@ -167,7 +189,7 @@
             lax.all_gather(ada_weight, "fsdp", axis=0, tiled=True),
             lax.all_gather(ada_bias, "fsdp", axis=0, tiled=True),
             lax.all_gather(attn_gain, "fsdp", axis=0, tiled=True),
-            lax.all_gather(qkv_weight, "fsdp", axis=0, tiled=True),
+            collect(qkv_weight, "fsdp", 0),
             lax.all_gather(out_weight, "fsdp", axis=0, tiled=True),
         )
 

time: 827 us -> 866 us (1.047)
  blocking collectives: 332 us -> 345 us
  local copies, waits for them, and re-layouts: 74.4 us -> 86.6 us
  other arithmetic: 28.6 us -> 39.5 us
    all_gather x1 -> x0, waiting for transfers between devices: 21.9 us -> none  [gather_attention(): lax.all_gather(qkv_weight, 'fsdp', axis=0, tiled=True)]
    ppermute x0 -> x3, waiting for transfers between devices: none -> 21.7 us  [the longest x2 21.7 us: collect(): lower.append(lax.ppermute(lower[-1] if lower else shard, axis, pairs))]
    unnamed x2, blocking collectives: 20 us -> 33.5 us
    unnamed x136 -> x128, local copies, waits for them, and re-layouts: 14.6 us -> 20.6 us
  transfers between devices with their start and end apart: 10 -> 12, of which waited for: 3 -> 3; matrix products, arithmetic and copies ran while one was open for 27% -> 28% of each run, Pallas kernels for 0% -> 0%
where the time goes in v1:
time: 866 us; the launch traced here: 857 us
  blocking collectives  345 us (40%)
  matrix products  264 us (30%)
  waiting for transfers between devices  101 us (12%)
  local copies, waits for them, and re-layouts  86.6 us (10%)
  other arithmetic  39.5 us (5%)
  between operations  17.3 us (2%)
    psum x1, blocking collectives, local(): lax.psum((mlp_shares[0], mlp_shares[1], mlp_shares[2], mlp_shares[3], mlp...  301 us
    reduce_scatter x1, waiting for transfers between devices, local(): lax.psum_scatter(down_weight_grad.astype(jnp.bfloat16), 'fsdp', scatter_d...  50.5 us
    dot_general x36, matrix products, head_scores(): jnp.dot(query_h, key_h.T, preferred_element_type=jnp.float32)  50.3 us
    dot_general x24, matrix products, attend_head(): jnp.dot(weights, value_h, preferred_element_type=jnp.float32)  38.8 us
    unnamed x2, blocking collectives  33.5 us
    dynamic_update_slice x24, local copies, waits for them, and re-layouts, run_forward(): head_out, row_max, row_total = lax.map(attend_head, (queries, keys, values))  32.2 us
    reduce_scatter x1, waiting for transfers between devices, local(): lax.psum_scatter(up_weight_grad.astype(jnp.bfloat16), 'fsdp', scatter_dim...  26.4 us
    dot_general x12, matrix products, head_grads(): jnp.dot(score_grad.T, query_h, preferred_element_type=jnp.float32)  23.3 us
  transfers between devices with their start and end apart: 12, of which 3 were waited for; matrix products, arithmetic and copies ran while one was open for 28% of the time, Pallas kernels for 0%

profile of v1, /device:TPU:0, one launch (start us, length us, event | category | flops | bytes accessed | tf_op | source)
XLA Modules:
  0.0 857.5 jit_solution(10456538921583791587)
XLA Ops:
  10.0 2.0 collective-permute-start.2
  19.8 22.7 %all-reduce.10 = (bf16[768]{0:T(1024)(128)(2,1)}, bf16[768]{0:T(1024)(128)(2,1)}, bf16[768]{0:T(1024)(128)(2,1)}) all-reduce(bf16[768]{0:T(1024)(128)(2,1)} %dynamic-update-slice, bf16[768]{0:T(1024)(128)(2,1)} %copy-done.47, bf16[768]{0:T(1024)(128)(2,1)S(1)} %dynamic-update-slice.1), channel_id=1, replica_groups=mesh['dp'=8,'fsdp'=4] {'fsdp'}, use_global_device_ids=true, to_apply=%add | all-reduce | flops 2304 | bytes 9216
  47.7 5.4 all-gather.1
  53.7 5.2 all-gather
  69.6 21.7 %collective-permute-done.1 = bf16[192,2304]{1,0:T(8,128)(2,1)} collective-permute-done((bf16[192,2304]{1,0:T(8,128)(2,1)S(1)}, bf16[192,2304]{1,0:T(8,128)(2,1)}, u32[]{:S(2)}, u32[]{:S(2)}) %collective-permute-start.1) | collective-permute-done | bytes 884768 | tf_op jit(solution)/shard_map/ppermute | solution.py:23
  91.3 3.2 pad_maximum_fusion
  94.5 4.7 gather_fusion
  99.3 4.5 fusion.111
  103.8 2.0 fusion.119
  109.0 2.7 copy.57
  111.7 2.9 copy.52
  114.6 2.0 subtract_convert_fusion.2
  120.1 2.6 copy.56
  122.7 73.9 %while.42 = (s32[]{:T(128)}, bf16[12,576,64]{1,2,0:T(8,128)(2,1)}, f32[12,576]{1,0:T(8,128)}, f32[12,576]{1,0:T(8,128)}, bf16[12,576,64]{2,1,0:T(8,128)(2,1)S(1)...) while((s32[]{:T(128)}, bf16[12,576,64]{1,2,0:T(8,128)(2,1)}, ...), condition=%wide.region_11.12_spmd.clone, body=%wide.region_8.11_spmd.sunk.clone | while | flops 87255936 | bytes 4619613 | solution.py:133
  191.9 1.9 fusion.193
  197.8 3.7 fusion.116
  202.5 7.6 fusion.114
  210.2 11.7 %fusion.123 = (bf16[3072]{0:T(1024)(128)(2,1)}, bf16[576,3072]{1,0:T(8,128)(2,1)S(1)}) fusion(f32[576,3072]{1,0:T(8,128)} %fusion.114, f32[3072]{0:T(1024)} %bitcast.214, bf16[3072,768]{1,0:T(8,128)(2,1)} %all-gather.13.cloned.1.call-done, bf16[576,768]{1,0:T(8,128)(2,1)S(1)} %copy-done.10, f32[768]{0:T(1024)} %get-tuple-element.214), kind=kOutput, calls=%fused_computation.207 | convolution fusion | flops 2758161408 | bytes 16241664 | tf_op jit(solution)/shard_map/dot_general | solution.py:237
  221.9 4.0 multiply_reduce_fusion.1
  228.0 2.3 convolution_convert_fusion.3
  230.3 3.7 convolution_convert_fusion.4
  234.0 2.3 copy.61
  236.2 113.5 %while.43 = (s32[]{:T(128)}, f32[12,576,64]{1,2,0:T(8,128)}, f32[12,576,64]{1,2,0:T(8,128)}, bf16[12,576,64]{1,2,0:T(8,128)(2,1)}, bf16[12,576,64]{2,1,0:T(8,128...) while((s32[]{:T(128)}, f32[12,576,64]{1,2,0:T(8,128)}, ...), condition=%wide.region_18.19_spmd.clone, body=%wide.region_16.18_spmd.sunk.clone | while | flops 215395776 | bytes 11369585 | solution.py:272
  241.9 1.9 fusion.204
  251.3 1.9 fusion.204
  260.8 1.9 fusion.204
  270.2 1.9 fusion.204
  279.7 1.9 fusion.204
  289.2 1.9 fusion.204
  298.6 1.9 fusion.204
  308.1 1.9 fusion.204
  317.5 1.9 fusion.204
  327.0 1.9 fusion.204
  345.9 1.9 fusion.204
  349.8 2.8 add_convert_fusion.4
  352.9 2.4 copy-done.9
  355.3 2.8 fusion.78
  359.9 3.1 multiply_reduce_fusion.3
  367.2 9.4 %fusion.76 = bf16[768]{0:T(1024)(128)(2,1)} fusion(bf16[576,768]{1,0:T(8,128)(2,1)S(1)} %copy-done.10, bf16[3072,768]{1,0:T(8,128)(2,1)} %all-gather.13.cloned.1.call-done, f32[768]{0:T(1024)} %convert_element_type.257, f32[576,3072]{1,0:T(8,128)} %fusion.114, f32[3072]{0:T(1024)} %bitcast.215), kind=kOutput, calls=%fused_computation.112 | convolution fusion | flops 2737372416 | bytes 12698112 | tf_op jit(solution)/shard_map/dot_general | solution.py:144
  379.4 6.9 convolution_convert_fusion
  387.0 7.9 convolution_convert_fusion.2
  398.0 10.5 %convolution_convert_fusion.1 = bf16[3072,768]{1,0:T(8,128)(2,1)} fusion(bf16[576,768]{1,0:T(8,128)(2,1)S(1)} %copy-done.10, f32[768]{0:T(1024)S(1)} %copy-done.34, f32[576,3072]{1,0:T(8,128)} %fusion.114, f32[3072]{0:T(1024)S(1)} %bitcast.216), kind=kOutput, calls=%fused_computation.85 | convolution fusion | flops 2739290112 | bytes 12696576 | tf_op jit(solution)/shard_map/dot_general | solution.py:235
  409.7 35.6 %while.41 = (s32[]{:T(128)}, bf16[12,576,64]{1,2,0:T(8,128)(2,1)S(1)}, bf16[12,576,64]{2,1,0:T(8,128)(2,1)}, bf16[12,576,64]{2,1,0:T(8,128)(2,1)}, bf16[12,576,64]{2,1,0:T(8,128)(2,1)}) while((s32[]{:T(128)}, bf16[12,576,64]{1,2,0:T(8,128)(2,1)S(1)}, bf16[12,576,64]{2,1,0:T(8,128)(2,1)}, bf16[12,576,64]{2,1,0:T(8,128)(2,1)}, ...), condition=%wide.region_5.6_spmd.clone, body=%wide.region_2.5_spmd.sunk.clone | while | flops 87255936 | bytes 4752197 | solution.py:133
  447.9 10.8 %all-reduce.9 = (bf16[4608]{0:T(1024)(128)(2,1)S(1)}, bf16[768]{0:T(1024)(128)(2,1)S(1)}, bf16[768]{0:T(1024)(128)(2,1)S(1)}, bf16[3072]{0:T(1024)(128)(2,1)S(1)}, bf16[768]{0:T(1024)(128)(2,1)S(1)}) all-reduce(bf16[4608]{0:T(1024)(128)(2,1)S(1)} %dynamic-update-slice.8, ...), channel_id=3, replica_groups=mesh['dp'=8,'fsdp'=4] {'fsdp'}, use_global_device_ids=true, to_apply=%region_29.30.clone | all-reduce | flops 9984 | bytes 39936
  460.1 12.4 %add_convert_fusion.1 = bf16[576,768]{1,0:T(8,128)(2,1)} fusion(f32[576,768]{1,0:T(8,128)} %copy-done.11, bf16[3072,768]{1,0:T(8,128)(2,1)} %all-gather.13.cloned.1.call-done, bf16[768,3072]{1,0:T(8,128)(2,1)} %all-gather.11.cloned.1.call-done, f32[3072]{0:T(1024)S(1)} %bitcast.217, f32[768]{0:T(1024)S(1)} %copy-done.49, f32[768]{0:T(1024)S(1)} %copy-done.50, ...), kind=kOutput, calls=%fused_computation.124 | convolution fusion | flops 5457936384 | bytes 12123648 | tf_op jit(solution)/shard_map/dot_general | solution.py:144
  472.5 26.4 %reduce-scatter.12.cloned.1.call-done = bf16[192,3072]{1,0:T(8,128)(2,1)} async-done(((bf16[768,3072]{1,0:T(8,128)(2,1)}), bf16[192,3072]{1,0:T(8,128)(2,1)}) %reduce-scatter.12.cloned.1.call-update) | async-done | bytes 1179664 | tf_op jit(solution)/shard_map/reduce_scatter | solution.py:252
  499.0 50.5 %reduce-scatter.14.cloned.1.call-done = bf16[768,768]{1,0:T(8,128)(2,1)} async-done(((bf16[3072,768]{1,0:T(8,128)(2,1)}), bf16[768,768]{1,0:T(8,128)(2,1)}) %reduce-scatter.14.cloned.1.call-update) | async-done | bytes 1179664 | tf_op jit(solution)/shard_map/reduce_scatter | solution.py:258
  549.5 301.2 %all-reduce.12 = (f32[32,4608]{1,0:T(8,128)}, f32[1152]{0:T(1024)}, f32[192]{0:T(256)}, f32[192,2304]{1,0:T(8,128)}, f32[192,768]{1,0:T(8,128)}, /*index=5*/f32[...) all-reduce(bf16[32,4608]{1,0:T(8,128)(2,1)} %reduce-scatter.6.clone, ...), channel_id=1, replica_groups=mesh['dp'=8,'fsdp'=4] {'dp'}, use_global_device_ids=true, to_apply=%region_28.29 | all-reduce | flops 1919424 | bytes 11521536 | tf_op jit(solution)/shard_map/psum | solution.py:309
  (405 shorter events, 252.2 us)
Async XLA Ops:
  7.2 2.3 copy-start.16
  7.2 59.4 %all-gather.7.cloned.1.call-start = ((), (), s32[]{:S(2)}) async-start(), calls=%async_computation.5 | async-start | bytes 1474560 | tf_op jit(solution)/shard_map/all_gather | solution.py:189
  7.9 188.7 %all-gather.9.cloned.1.call-start = ((), (), s32[]{:S(2)}) async-start(), calls=%async_computation.6 | async-start | bytes 1474560 | tf_op jit(solution)/shard_map/all_gather | solution.py:193
  8.7 193.8 %all-gather.11.cloned.1.call-start = ((), (), s32[]{:S(2)}) async-start(), calls=%async_computation.7 | async-start | bytes 5898240 | tf_op jit(solution)/shard_map/all_gather | solution.py:199
  9.4 200.7 %all-gather.13.cloned.1.call-start = ((), (), s32[]{:S(2)}) async-start(), calls=%async_computation.8 | async-start | bytes 5898240 | tf_op jit(solution)/shard_map/all_gather | solution.py:201
  9.5 53.5 %collective-permute-start = (bf16[192,2304]{1,0:T(8,128)(2,1)S(1)}, bf16[192,2304]{1,0:T(8,128)(2,1)S(1)}, u32[]{:S(2)}, u32[]{:S(2)}) collective-permute-start(bf16[192,2304]{1,0:T(8,128)(2,1)S(1)} %copy-done.16), channel_id=1, source_target_pairs={{0,1},{1,2},{2,3},{3,0},{4,5},{5,6},{6,7},{7,4},{8,9},{9,10},{10,1... | collective-permute-start | bytes 2654216 | tf_op jit(solution)/shard_map/ppermute | solution.py:23
  10.0 59.6 %collective-permute-start.2 = (bf16[192,2304]{1,0:T(8,128)(2,1)S(1)}, bf16[192,2304]{1,0:T(8,128)(2,1)S(1)}, u32[]{:S(2)}, u32[]{:S(2)}) collective-permute-start(bf16[192,2304]{1,0:T(8,128)(2,1)S(1)} %copy-done.16), channel_id=1, source_target_pairs={{1,0},{2,1},{3,2},{0,3},{5,4},{6,5},{7,6},{4,7},{9,8},{10,9},{11,1... | collective-permute-start | bytes 2654216 | tf_op jit(solution)/shard_map/ppermute | solution.py:25
  12.0 460.5 %reduce-scatter.10.cloned.1.call-start = ((), (), s32[]{:S(2)}) async-start(), calls=%async_computation.11 | async-start | bytes 1474560 | tf_op jit(solution)/shard_map/reduce_scatter | solution.py:305
  12.7 2.2 copy-start.52
  12.8 48.8 %copy-start = (bf16[576,768]{1,0:T(8,128)(2,1)S(1)}, bf16[576,768]{1,0:T(8,128)(2,1)}, u32[]{:S(2)}) copy-start(bf16[576,768]{1,0:T(8,128)(2,1)} %param.19) | copy-start | bytes 2654212
  63.0 28.4 %collective-permute-start.1 = (bf16[192,2304]{1,0:T(8,128)(2,1)S(1)}, bf16[192,2304]{1,0:T(8,128)(2,1)}, u32[]{:S(2)}, u32[]{:S(2)}) collective-permute-start(bf16[192,2304]{1,0:T(8,128)(2,1)S(1)} %collective-permute-done), channel_id=1, source_target_pairs={{0,1},{1,2},{2,3},{3,0},{4,5},{5,6},{6,7},{7,4},{8,9},{9,10},{10,1... | collective-permute-start | bytes 2654216 | tf_op jit(solution)/shard_map/ppermute | solution.py:23
  94.5 4.7 copy-start.19
  94.5 4.7 copy-start.21
  94.5 4.7 copy-start.23
  94.5 4.7 copy-start.51
  111.7 2.9 copy-start.17
  111.7 2.9 copy-start.18
  122.7 75.1 %copy-start.35 = (f32[768]{0:T(1024)S(1)}, f32[768]{0:T(1024)}, u32[]{:S(2)}) copy-start(f32[768]{0:T(1024)} %get-tuple-element.219) | copy-start | bytes 9220
  202.5 7.6 copy-start.10
  210.1 11.7 %copy-start.30 = (f32[576]{0:T(1024)S(1)}, f32[576]{0:T(1024)}, u32[]{:S(2)}) copy-start(f32[576]{0:T(1024)} %copy-done.29) | copy-start | bytes 6916
  210.1 11.7 %copy-start.38 = (f32[768]{0:T(1024)S(1)}, f32[768]{0:T(1024)}, u32[]{:S(2)}) copy-start(f32[768]{0:T(1024)} %convert_element_type.253) | copy-start | bytes 9220
  210.1 11.7 %copy-start.40 = (f32[576]{0:T(1024)S(1)}, f32[576]{0:T(1024)}, u32[]{:S(2)}) copy-start(f32[576]{0:T(1024)} %fusion.98) | copy-start | bytes 6916
  210.1 11.7 %copy-start.41 = (f32[768]{0:T(1024)S(1)}, f32[768]{0:T(1024)}, u32[]{:S(2)}) copy-start(f32[768]{0:T(1024)} %get-tuple-element.216) | copy-start | bytes 9220
  210.2 11.7 %copy-start.54 = (bf16[768,3072]{1,0:T(8,128)(2,1)S(1)}, bf16[768,3072]{1,0:T(8,128)(2,1)}, u32[]{:S(2)}) copy-start(bf16[768,3072]{1,0:T(8,128)(2,1)} %all-gather.11.cloned.1.call-done) | copy-start | bytes 14155780
  221.8 4.1 copy-start.55
  221.9 4.1 copy-start.28
  349.7 122.8 %reduce-scatter.6.cloned.1.call-start = ((), (), s32[]{:S(2)}) async-start(), calls=%async_computation.9 | async-start | bytes 1474560 | tf_op jit(solution)/shard_map/reduce_scatter | solution.py:293
  349.8 3.1 copy-start.13
  352.6 2.7 copy-start.9
  352.6 2.7 copy-start.20
  352.6 2.7 copy-start.24
  352.7 5.3 copy-start.14
  352.9 5.2 copy-start.15
  355.3 2.8 copy-start.26
  355.3 2.8 copy-start.22
  355.3 4.6 copy-start.6
  379.4 93.2 %reduce-scatter.8.cloned.1.call-start = ((), (), s32[]{:S(2)}) async-start(), calls=%async_computation.10 | async-start | bytes 4423680 | tf_op jit(solution)/shard_map/reduce_scatter | solution.py:302
  386.4 112.6 %reduce-scatter.12.cloned.1.call-start = ((), (), s32[]{:S(2)}) async-start(), calls=%async_computation.12 | async-start | bytes 5898240 | tf_op jit(solution)/shard_map/reduce_scatter | solution.py:252
  395.0 3.0 copy-start.43
  395.0 154.5 %reduce-scatter.14.cloned.1.call-start = ((), (), s32[]{:S(2)}) async-start(), calls=%async_computation.13 | async-start | bytes 5898240 | tf_op jit(solution)/shard_map/reduce_scatter | solution.py:258
  409.7 35.6 %copy-start.12 = (bf16[768,768]{1,0:T(8,128)(2,1)S(1)}, bf16[768,768]{1,0:T(8,128)(2,1)}, u32[]{:S(2)}) copy-start(bf16[768,768]{1,0:T(8,128)(2,1)} %all-gather.9.cloned.1.call-done) | copy-start | bytes 3538948
  409.7 35.6 %copy-start.37 = (f32[768]{0:T(1024)S(1)}, f32[768]{0:T(1024)}, u32[]{:S(2)}) copy-start(f32[768]{0:T(1024)} %get-tuple-element.219) | copy-start | bytes 9220
  446.4 12.7 %copy-start.7 = (bf16[128,4608]{1,0:T(8,128)(2,1)S(1)}, bf16[128,4608]{1,0:T(8,128)(2,1)}, u32[]{:S(2)}) copy-start(bf16[128,4608]{1,0:T(8,128)(2,1)} %all-gather.7.cloned.1.call-done) | copy-start | bytes 3538948
  446.4 13.7 %copy-start.39 = (f32[768]{0:T(1024)S(1)}, f32[768]{0:T(1024)}, u32[]{:S(2)}) copy-start(f32[768]{0:T(1024)} %convert_element_type.253) | copy-start | bytes 9220
  446.4 13.7 %copy-start.42 = (f32[768]{0:T(1024)S(1)}, f32[768]{0:T(1024)}, u32[]{:S(2)}) copy-start(f32[768]{0:T(1024)} %get-tuple-element.216) | copy-start | bytes 9220
  446.4 13.7 %copy-start.44 = (f32[4,1,768]{2,1,0:T(1,128)S(1)}, f32[4,1,768]{2,1,0:T(1,128)}, u32[]{:S(2)}) copy-start(f32[4,1,768]{2,1,0:T(1,128)} %convert_element_type.288) | copy-start | bytes 36868
  446.4 13.6 %copy-start.49 = (f32[768]{0:T(1024)S(1)}, f32[768]{0:T(1024)}, u32[]{:S(2)}) copy-start(f32[768]{0:T(1024)} %convert_element_type.257) | copy-start | bytes 9220
  446.4 13.6 %copy-start.50 = (f32[768]{0:T(1024)S(1)}, f32[768]{0:T(1024)}, u32[]{:S(2)}) copy-start(f32[768]{0:T(1024)} %get-tuple-element.215) | copy-start | bytes 9220
  (20 other events, 27.1 us)
Sparse Core Ops, SparseCore 0:
  9.6 26.6 all-gather.6
  37.8 17.5 all-gather.8
  56.9 45.3 all-gather.10
  103.8 37.5 all-gather.12
  349.9 25.8 reduce-scatter.9
  379.5 25.9 reduce-scatter.5
  408.0 40.3 reduce-scatter.7
  451.0 47.9 reduce-scatter.11
  501.5 47.9 reduce-scatter.13
